TPU v7x, 32 devices: a whole 2x2x4 slice. The times are simulated.
32 devices in a mesh: tp: 8 (over y, x, core), dp: 4 (over z).
Axes of the slice: x: 2, y: 2, z: 4, core: 2. Of those that a mesh axis runs over, the one named last changes fastest.
Arguments:
- activations: bfloat16 [64, 512, 4096], P('dp', None, 'tp'), may hold values from -6 to 6
- query_output_cotangent: bfloat16 [64, 512, 4096], P('dp', None, 'tp'), may hold values from -6 to 6
- value_output_cotangent: bfloat16 [64, 512, 4096], P('dp', None, 'tp'), may hold values from -6 to 6
- lengths: int32 [64], P('dp'), may hold values from 1 to 512
- reducing_matrices_pair: bfloat16 [2, 4096, 128], P(None, 'tp'), may hold values from -0.09375 to 0.09375
- expanding_matrices_pair: bfloat16 [2, 128, 4096], P(None, None, 'tp'), may hold values from -0.5 to 0.5
- width_side_projections: bfloat16 [2, 4096, 128], P(None, 'tp'), may hold values from -0.09375 to 0.09375
- narrow_random_sketch: bfloat16 [128, 16], replicated, may hold values from -0.5 to 0.5
- projected_first_moment: float32 [8192], replicated, may hold values from -6 to 6
- projected_second_moment: float32 [8192], replicated, may hold values from 0.1 to 10
- targets: bfloat16 [1024, 8192], P('dp', 'tp'), may hold values from -6 to 6
Outputs:
- scores: float32 [64, 1024], P('dp', 'tp')
All inputs are finite; a program needn't handle non-finite values.
Results may differ from a plain program's by a relative error of at most 0.023.
Values may be sent and summed in bfloat16 or wider, within the bound.
A program may use at most 128 MiB of HBM per device.

v0:
```python
import math
import jax
import jax.numpy as jnp
from jax import lax
from jax.sharding import PartitionSpec as P


def adam_update(features, first_moment, second_moment):
    mixed = 0.9 * first_moment + 0.1 * features
    spread = 0.999 * second_moment + 0.001 * features * features
    return mixed / (jnp.sqrt(spread) + 1e-08)


def combine_factors(reducing_matrices_pair, expanding_matrices_pair, narrow_random_sketch):
    attention_key_reducer = jnp.dot(
        reducing_matrices_pair[0], narrow_random_sketch, preferred_element_type=jnp.float32
    ).astype(jnp.bfloat16)
    value_down_factor = jnp.dot(
        reducing_matrices_pair[1], narrow_random_sketch, preferred_element_type=jnp.float32
    ).astype(jnp.bfloat16)
    query_up_factor = jnp.dot(
        expanding_matrices_pair[0].T, narrow_random_sketch, preferred_element_type=jnp.float32
    ).astype(jnp.bfloat16)
    value_up_factor = jnp.dot(
        expanding_matrices_pair[1].T, narrow_random_sketch, preferred_element_type=jnp.float32
    ).astype(jnp.bfloat16)
    return (attention_key_reducer, value_down_factor, query_up_factor, value_up_factor)


def body(
    activations,
    query_output_cotangent,
    value_output_cotangent,
    lengths,
    reducing_matrices_pair,
    expanding_matrices_pair,
    width_side_projections,
    narrow_random_sketch,
    projected_first_moment,
    projected_second_moment,
    targets,
):
    attention_key_reducer, value_down_factor, query_up_factor, value_up_factor = combine_factors(
        reducing_matrices_pair, expanding_matrices_pair, narrow_random_sketch
    )
    rank_cols = narrow_random_sketch.shape[1]
    w_left = jnp.concatenate(
        [attention_key_reducer, value_down_factor, width_side_projections[0]], axis=1
    )
    w_query = jnp.concatenate([query_up_factor, width_side_projections[1]], axis=1)
    w_value = jnp.concatenate([value_up_factor, width_side_projections[1]], axis=1)
    groups = lax.axis_size("tp")
    parts = lax.axis_size("dp")
    member = lax.axis_index("tp")
    local_ex, seq_len = activations.shape[:2]
    feature_count = projected_first_moment.shape[0]
    positions = jnp.arange(seq_len, dtype=jnp.int32)
    token_mask = (positions[None, :] < lengths[:, None])[..., None]

    def project(rows, weights):
        out = jnp.einsum("esd,dc->esc", rows, weights, preferred_element_type=jnp.float32)
        return out.astype(jnp.bfloat16)

    left = project(activations, w_left)
    right_q = project(query_output_cotangent, w_query)
    right_v = project(value_output_cotangent, w_value)
    narrow = jnp.concatenate(
        [left[..., : 2 * rank_cols], right_q[..., :rank_cols], right_v[..., :rank_cols]], axis=-1
    )
    narrow = jnp.where(token_mask, narrow, jnp.zeros((), jnp.bfloat16))
    narrow = lax.psum(narrow, "tp")

    def outer_sum(first, wide):
        return jnp.einsum(
            "esr,esk->erk",
            narrow[..., first * rank_cols : (first + 1) * rank_cols],
            wide,
            preferred_element_type=jnp.float32,
        )

    own_features = jnp.concatenate(
        [
            outer_sum(2, left[..., 2 * rank_cols :]),
            outer_sum(3, left[..., 2 * rank_cols :]),
            outer_sum(0, right_q[..., rank_cols:]),
            outer_sum(1, right_v[..., rank_cols:]),
        ],
        axis=1,
    ).reshape(local_ex, -1)
    features = lax.psum_scatter(
        own_features.astype(jnp.bfloat16), "tp", scatter_dimension=1, tiled=True
    ).astype(jnp.float32)
    span = feature_count // groups
    first_moment = lax.dynamic_slice_in_dim(projected_first_moment, member * span, span)
    second_moment = lax.dynamic_slice_in_dim(projected_second_moment, member * span, span)
    update = adam_update(features, first_moment, second_moment).astype(jnp.bfloat16)
    update = lax.all_gather(update, "dp", axis=0, tiled=True)
    wide_update = update.astype(jnp.float32)
    target_float = targets.astype(jnp.float32)
    update_sq = jnp.sum(wide_update * wide_update, axis=1)
    target_sq = jnp.sum(target_float * target_float, axis=1)
    dots = lax.dot_general(
        update, targets, (((1,), (1,)), ((), ())), preferred_element_type=jnp.float32
    )
    rows = jnp.concatenate(
        [dots, jnp.broadcast_to(update_sq[:, None], (dots.shape[0], 128))], axis=1
    ).reshape(parts, local_ex, -1)
    extra = jnp.pad(target_sq, (0, 128))
    rows = jnp.concatenate([rows, jnp.broadcast_to(extra, (parts, 8, extra.shape[0]))], axis=1)
    rows = lax.psum(rows, "tp")
    rows = lax.all_to_all(rows, "dp", split_axis=0, concat_axis=0, tiled=True)
    owned = targets.shape[0]
    totals = jnp.moveaxis(rows[:, :, :owned], 0, 1).reshape(local_ex + 8, parts * owned)
    columns = parts * owned // groups
    totals = lax.dynamic_slice_in_dim(totals, member * columns, columns, 1)
    row_scale = lax.rsqrt(rows[0, :local_ex, owned : owned + 1] + 1e-06)
    column_scale = lax.rsqrt(totals[local_ex : local_ex + 1] + 1e-06)
    return totals[:local_ex] * row_scale * column_scale * math.sqrt(feature_count)


def solution(mesh):
    placed = (
        P("dp", None, "tp"),
        P("dp", None, "tp"),
        P("dp", None, "tp"),
        P("dp"),
        P(None, "tp", None),
        P(None, None, "tp"),
        P(None, "tp", None),
        P(),
        P(),
        P(),
        P("dp", "tp"),
    )
    return jax.shard_map(body, mesh=mesh, in_specs=placed, out_specs=P("dp", "tp"), check_vma=False)
```

profile of v0, /device:TPU:0, one launch (start us, length us, event | category | flops | bytes accessed | tf_op | source)
XLA Modules:
  0.0 220.2 jit_solution(16352123582546980845)
XLA Ops:
  6.5 0.7 copy-done
  7.2 1.0 convolution_convert_fusion.2
  8.3 1.1 convolution_convert_fusion.3
  9.3 1.0 convolution_convert_fusion.1
  10.4 1.0 convolution_convert_fusion
  11.4 1.0 fusion.55
  12.5 6.3 %convert_bitcast_fusion = bf16[16,512,160]{1,2,0:T(8,128)(2,1)S(1)} fusion(bf16[16,512,512]{2,1,0:T(8,128)(2,1)} %param.11, bf16[512,128]{0,1:T(8,128)(2,1)S(1)} %bitcast.53, bf16[512,16]{0,1:T(8,128)(2,1)S(1)} %convolution_convert_fusion.2, bf16[512,16]{0,1:T(8,128)(2,1)S(1)} %convolution_convert_fusion.3), kind=kOutput, calls=%fused_computation | convolution fusion | flops 1343979520 | bytes 11173888 | tf_op jit(solution)/shard_map/esd,dc->esc/dot_general | solution.py:61
  18.9 7.1 %convert_bitcast_fusion.2 = bf16[16,512,144]{1,2,0:T(8,128)(2,1)S(1)} fusion(bf16[16,512,512]{2,1,0:T(8,128)(2,1)} %param.12, bf16[512,16]{0,1:T(8,128)(2,1)S(1)} %convolution_convert_fusion.1, bf16[512,128]{0,1:T(8,128)(2,1)S(1)} %bitcast.49), kind=kOutput, calls=%fused_computation.2 | convolution fusion | flops 1209434112 | bytes 10895360 | tf_op jit(solution)/shard_map/esd,dc->esc/dot_general | solution.py:61
  26.1 7.1 %convert_bitcast_fusion.1 = bf16[16,512,144]{1,2,0:T(8,128)(2,1)S(1)} fusion(bf16[16,512,512]{2,1,0:T(8,128)(2,1)} %param.13, bf16[512,16]{0,1:T(8,128)(2,1)S(1)} %convolution_convert_fusion, bf16[512,128]{0,1:T(8,128)(2,1)S(1)} %bitcast.50), kind=kOutput, calls=%fused_computation.1 | convolution fusion | flops 1209434112 | bytes 10895360 | tf_op jit(solution)/shard_map/esd,dc->esc/dot_general | solution.py:61
  33.2 1.4 copy-done.5
  34.7 1.3 maximum_select_fusion
  36.1 59.4 %all-reduce.4.cloned.1.call-done = bf16[16,512,64]{1,2,0:T(8,128)(2,1)} async-done(((bf16[16,512,64]{1,2,0:T(8,128)(2,1)}), bf16[16,512,64]{1,2,0:T(8,128)(2,1)}) %all-reduce.4.cloned.1.call-update) | async-done | bytes 1048592 | tf_op jit(solution)/shard_map/psum | solution.py:71
  95.5 1.7 fusion.8
  97.2 1.8 fusion.11
  100.4 0.9 copy.42
  101.5 0.7 dynamic-slice_multiply_fusion.1
  102.2 31.9 %reduce-scatter.2.cloned.1.call-done = bf16[16,1024]{1,0:T(8,128)(2,1)} async-done(((bf16[16,8192]{1,0:T(8,128)(2,1)}), bf16[16,1024]{1,0:T(8,128)(2,1)}) %reduce-scatter.2.cloned.1.call-update) | async-done | bytes 32784 | tf_op jit(solution)/shard_map/reduce_scatter | solution.py:90
  134.1 0.8 fusion.42
  134.9 13.5 %all_gather.3 = bf16[64,1024]{1,0:T(8,128)(2,1)S(1)} all-gather(bf16[16,1024]{1,0:T(8,128)(2,1)S(1)} %fusion.42), channel_id=1, replica_groups=mesh['tp'=8,'dp'=4] {'dp'}, dimensions={0}, use_global_device_ids=true | all-gather | bytes 163840 | tf_op jit(solution)/shard_map/all_gather | solution.py:97
  148.9 0.7 pad_maximum_fusion.1
  149.6 52.0 %all-reduce.6.cloned.1.call-done = f32[4,24,384]{2,1,0:T(8,128)} async-done(((f32[4,24,384]{2,1,0:T(8,128)}), f32[4,24,384]{2,1,0:T(8,128)}) %all-reduce.6.cloned.1.call-update) | async-done | bytes 147472 | tf_op jit(solution)/shard_map/psum | solution.py:110
  201.6 4.6 %all-to-all-start = ((f32[4,24,384]{2,1,0:T(8,128)}), f32[4,24,384]{2,1,0:T(8,128)S(1)}, u32[]{:S(2)}, u32[]{:S(2)}) async-start(f32[4,24,384]{2,1,0:T(8,128)} %all-reduce.6.cloned.1.call-done), calls=%async_computation.1 | async-start | bytes 294912 | tf_op jit(solution)/shard_map/all_to_all | solution.py:111
  206.2 6.6 %all-to-all-done = f32[4,24,384]{2,1,0:T(8,128)S(1)} async-done(((f32[4,24,384]{2,1,0:T(8,128)}), f32[4,24,384]{2,1,0:T(8,128)S(1)}, u32[]{:S(2)}, u32[]{:S(2)}) %all-to-all-start) | async-done | bytes 147488 | tf_op jit(solution)/shard_map/all_to_all | solution.py:111
  213.0 0.7 fusion.49
  (45 shorter events, 2.7 us)
Async XLA Ops:
  6.5 0.7 copy-start
  6.5 88.9 %all-reduce.4.cloned.1.call-start = ((), (), s32[]{:S(2)}) async-start(), calls=%async_computation.2 | async-start | bytes 2097152 | tf_op jit(solution)/shard_map/psum | solution.py:71
  18.8 7.2 %copy-start.1 = (bf16[16,512,160]{1,2,0:T(8,128)(2,1)}, bf16[16,512,160]{1,2,0:T(8,128)(2,1)S(1)}, u32[]{:S(2)}) copy-start(bf16[16,512,160]{1,2,0:T(8,128)(2,1)S(1)} %convert_bitcast_fusion) | copy-start | bytes 7864324
  26.0 7.2 %copy-start.3 = (bf16[16,512,144]{1,2,0:T(8,128)(2,1)}, bf16[16,512,144]{1,2,0:T(8,128)(2,1)S(1)}, u32[]{:S(2)}) copy-start(bf16[16,512,144]{1,2,0:T(8,128)(2,1)S(1)} %convert_bitcast_fusion.2) | copy-start | bytes 7077892
  26.1 8.6 %copy-start.8 = (s32[16]{0:T(128)S(1)}, s32[16]{0:T(128)}, u32[]{:S(2)}) copy-start(s32[16]{0:T(128)} %param.14) | copy-start | bytes 196
  26.1 8.6 %slice-start = ((bf16[16,512,160]{1,2,0:T(8,128)(2,1)}), bf16[16,512,32]{1,2,0:T(8,128)(2,1)S(1)}, s32[]{:S(2)}) async-start(bf16[16,512,160]{1,2,0:T(8,128)(2,1)} %copy-done.1), calls=%async_computation.5 | async-start | bytes 1048576 | tf_op jit(solution)/shard_map/slice | solution.py:68
  33.2 1.4 copy-start.5
  33.2 62.3 %copy-start.2 = (bf16[16,512,160]{1,2,0:T(8,128)(2,1)S(1)}, bf16[16,512,160]{1,2,0:T(8,128)(2,1)}, u32[]{:S(2)}) copy-start(bf16[16,512,160]{1,2,0:T(8,128)(2,1)} %copy-done.1) | copy-start | bytes 7864324
  36.0 98.1 %reduce-scatter.2.cloned.1.call-start = ((), (), s32[]{:S(2)}) async-start(), calls=%async_computation.3 | async-start | bytes 294912 | tf_op jit(solution)/shard_map/reduce_scatter | solution.py:90
  95.5 3.5 %copy-start.4 = (bf16[16,512,144]{1,2,0:T(8,128)(2,1)S(1)}, bf16[16,512,144]{1,2,0:T(8,128)(2,1)}, u32[]{:S(2)}) copy-start(bf16[16,512,144]{1,2,0:T(8,128)(2,1)} %copy-done.3) | copy-start | bytes 7077892
  95.5 3.5 %copy-start.9 = (bf16[16,512,64]{1,2,0:T(8,128)(2,1)S(1)}, bf16[16,512,64]{1,2,0:T(8,128)(2,1)}, u32[]{:S(2)}) copy-start(bf16[16,512,64]{1,2,0:T(8,128)(2,1)} %all-reduce.4.cloned.1.call-done) | copy-start | bytes 3145732
  97.2 2.4 %copy-start.6 = (bf16[16,512,144]{1,2,0:T(8,128)(2,1)S(1)}, bf16[16,512,144]{1,2,0:T(8,128)(2,1)}, u32[]{:S(2)}) copy-start(bf16[16,512,144]{1,2,0:T(8,128)(2,1)} %copy-done.5) | copy-start | bytes 7077892
  99.0 2.3 %copy-start.7 = (bf16[256,1024]{1,0:T(8,128)(2,1)S(1)}, bf16[256,1024]{1,0:T(8,128)(2,1)}, u32[]{:S(2)}) copy-start(bf16[256,1024]{1,0:T(8,128)(2,1)} %param.21) | copy-start | bytes 1572868
  101.3 100.4 %all-reduce.6.cloned.1.call-start = ((), (), s32[]{:S(2)}) async-start(), calls=%async_computation.4 | async-start | bytes 294912 | tf_op jit(solution)/shard_map/psum | solution.py:110
  201.6 11.2 %all-to-all-start = ((f32[4,24,384]{2,1,0:T(8,128)}), f32[4,24,384]{2,1,0:T(8,128)S(1)}, u32[]{:S(2)}, u32[]{:S(2)}) async-start(f32[4,24,384]{2,1,0:T(8,128)} %all-reduce.6.cloned.1.call-done), calls=%async_computation.1 | async-start | bytes 294912 | tf_op jit(solution)/shard_map/all_to_all | solution.py:111
Sparse Core Ops, SparseCore 0:
  36.1 59.2 all-reduce.3
  101.4 32.6 reduce-scatter.1
  149.8 51.8 all-reduce.5
where the time goes:
time: 221 us; the launch traced here: 220 us
  waiting for transfers between devices  150 us (68%)
  matrix products  29.7 us (13%)
  blocking collectives  13.5 us (6%)
  between operations  13.3 us (6%)
  other arithmetic  4.71 us (2%)
  starting transfers between devices  4.69 us (2%)
  local copies, waits for them, and re-layouts  4.36 us (2%)
    psum x1, waiting for transfers between devices, body(): narrow = lax.psum(narrow, 'tp')  59.4 us
    psum x1, waiting for transfers between devices, body(): rows = lax.psum(rows, 'tp')  52 us
    reduce_scatter x1, waiting for transfers between devices, body(): lax.psum_scatter(own_features.astype(jnp.bfloat16), 'tp', scatter_dimensi...  31.9 us
    dot_general x3, matrix products, project(): jnp.einsum('esd,dc->esc', rows, weights, preferred_element_type=jnp.float32)  20.4 us
    all_gather x1, blocking collectives, body(): update = lax.all_gather(update, 'dp', axis=0, tiled=True)  13.5 us
    all_to_all x1, waiting for transfers between devices, body(): rows = lax.all_to_all(rows, 'dp', split_axis=0, concat_axis=0, tiled=True)  6.65 us
    dot_general x4, matrix products, outer_sum(): jnp.einsum('esr,esk->erk', narrow[..., first * rank_cols:(first + 1) * ra...  4.82 us
    all_to_all x1, starting transfers between devices, body(): rows = lax.all_to_all(rows, 'dp', split_axis=0, concat_axis=0, tiled=True)  4.6 us
  transfers between devices with their start and end apart: 4, of which 4 were waited for; matrix products, arithmetic and copies ran while one was open for 0% of the time, Pallas kernels for 0%

commit v1 on v0

--- a/solution.py
+++ b/solution.py
@@ -107,7 +107,7 @@
     ).reshape(parts, local_ex, -1)
     extra = jnp.pad(target_sq, (0, 128))
     rows = jnp.concatenate([rows, jnp.broadcast_to(extra, (parts, 8, extra.shape[0]))], axis=1)
-    rows = lax.psum(rows, "tp")
+    rows = jnp.sum(lax.all_gather(rows, "tp"), axis=0)
     rows = lax.all_to_all(rows, "dp", split_axis=0, concat_axis=0, tiled=True)
     owned = targets.shape[0]
     totals = jnp.moveaxis(rows[:, :, :owned], 0, 1).reshape(local_ex + 8, parts * owned)

time: 221 us -> 195 us (0.88)
  waiting for transfers between devices: 150 us -> 122 us
    psum x1 -> x0, waiting for transfers between devices: 52 us -> none  [body(): rows = lax.psum(rows, 'tp')]
    all_gather x0 -> x1, waiting for transfers between devices: none -> 24.1 us  [body(): rows = jnp.sum(lax.all_gather(rows, 'tp'), axis=0)]
where the time goes in v1:
time: 195 us; the launch traced here: 194 us
  waiting for transfers between devices  122 us (63%)
  matrix products  29.7 us (15%)
  blocking collectives  13.5 us (7%)
  between operations  13.3 us (7%)
  other arithmetic  6.71 us (3%)
  starting transfers between devices  4.68 us (2%)
  local copies, waits for them, and re-layouts  4.36 us (2%)
    psum x1, waiting for transfers between devices, body(): narrow = lax.psum(narrow, 'tp')  59.4 us
    reduce_scatter x1, waiting for transfers between devices, body(): lax.psum_scatter(own_features.astype(jnp.bfloat16), 'tp', scatter_dimensi...  31.9 us
    all_gather x1, waiting for transfers between devices, body(): rows = jnp.sum(lax.all_gather(rows, 'tp'), axis=0)  24.1 us
    dot_general x3, matrix products, project(): jnp.einsum('esd,dc->esc', rows, weights, preferred_element_type=jnp.float32)  20.4 us
    all_gather x1, blocking collectives, body(): update = lax.all_gather(update, 'dp', axis=0, tiled=True)  13.5 us
    all_to_all x1, waiting for transfers between devices, body(): rows = lax.all_to_all(rows, 'dp', split_axis=0, concat_axis=0, tiled=True)  6.57 us
    dot_general x4, matrix products, outer_sum(): jnp.einsum('esr,esk->erk', narrow[..., first * rank_cols:(first + 1) * ra...  4.83 us
    all_to_all x1, starting transfers between devices, body(): rows = lax.all_to_all(rows, 'dp', split_axis=0, concat_axis=0, tiled=True)  4.6 us
  transfers between devices with their start and end apart: 4, of which 4 were waited for; matrix products, arithmetic and copies ran while one was open for 0% of the time, Pallas kernels for 0%

profile of v1, /device:TPU:0, one launch (start us, length us, event | category | flops | bytes accessed | tf_op | source)
XLA Modules:
  0.0 194.3 jit_solution(7509525870104352613)
XLA Ops:
  6.5 0.7 copy-done
  7.2 1.0 convolution_convert_fusion.2
  8.3 1.1 convolution_convert_fusion.3
  9.3 1.0 convolution_convert_fusion.1
  10.4 1.0 convolution_convert_fusion
  11.4 1.0 fusion.55
  12.5 6.3 %convert_bitcast_fusion = bf16[16,512,160]{1,2,0:T(8,128)(2,1)S(1)} fusion(bf16[16,512,512]{2,1,0:T(8,128)(2,1)} %param.11, bf16[512,128]{0,1:T(8,128)(2,1)S(1)} %bitcast.55, bf16[512,16]{0,1:T(8,128)(2,1)S(1)} %convolution_convert_fusion.2, bf16[512,16]{0,1:T(8,128)(2,1)S(1)} %convolution_convert_fusion.3), kind=kOutput, calls=%fused_computation | convolution fusion | flops 1343979520 | bytes 11173888 | tf_op jit(solution)/shard_map/esd,dc->esc/dot_general | solution.py:61
  18.9 7.1 %convert_bitcast_fusion.2 = bf16[16,512,144]{1,2,0:T(8,128)(2,1)S(1)} fusion(bf16[16,512,512]{2,1,0:T(8,128)(2,1)} %param.12, bf16[512,16]{0,1:T(8,128)(2,1)S(1)} %convolution_convert_fusion.1, bf16[512,128]{0,1:T(8,128)(2,1)S(1)} %bitcast.50), kind=kOutput, calls=%fused_computation.2 | convolution fusion | flops 1209434112 | bytes 10895360 | tf_op jit(solution)/shard_map/esd,dc->esc/dot_general | solution.py:61
  26.1 7.1 %convert_bitcast_fusion.1 = bf16[16,512,144]{1,2,0:T(8,128)(2,1)S(1)} fusion(bf16[16,512,512]{2,1,0:T(8,128)(2,1)} %param.13, bf16[512,16]{0,1:T(8,128)(2,1)S(1)} %convolution_convert_fusion, bf16[512,128]{0,1:T(8,128)(2,1)S(1)} %bitcast.51), kind=kOutput, calls=%fused_computation.1 | convolution fusion | flops 1209434112 | bytes 10895360 | tf_op jit(solution)/shard_map/esd,dc->esc/dot_general | solution.py:61
  33.2 1.4 copy-done.5
  34.7 1.3 maximum_select_fusion
  36.1 59.4 %all-reduce.3.cloned.1.call-done = bf16[16,512,64]{1,2,0:T(8,128)(2,1)} async-done(((bf16[16,512,64]{1,2,0:T(8,128)(2,1)}), bf16[16,512,64]{1,2,0:T(8,128)(2,1)}) %all-reduce.3.cloned.1.call-update) | async-done | bytes 1048592 | tf_op jit(solution)/shard_map/psum | solution.py:71
  95.5 1.7 fusion.8
  97.2 1.8 fusion.11
  100.4 0.9 copy.41
  101.5 0.7 dynamic-slice_multiply_fusion.1
  102.2 31.9 %reduce-scatter.2.cloned.1.call-done = bf16[16,1024]{1,0:T(8,128)(2,1)} async-done(((bf16[16,8192]{1,0:T(8,128)(2,1)}), bf16[16,1024]{1,0:T(8,128)(2,1)}) %reduce-scatter.2.cloned.1.call-update) | async-done | bytes 32784 | tf_op jit(solution)/shard_map/reduce_scatter | solution.py:90
  134.1 0.8 fusion.42
  134.9 13.5 %all_gather.9 = bf16[64,1024]{1,0:T(8,128)(2,1)S(1)} all-gather(bf16[16,1024]{1,0:T(8,128)(2,1)S(1)} %fusion.42), channel_id=1, replica_groups=mesh['tp'=8,'dp'=4] {'dp'}, dimensions={0}, use_global_device_ids=true | all-gather | bytes 163840 | tf_op jit(solution)/shard_map/all_gather | solution.py:97
  149.6 24.1 %all-gather.3.cloned.1.call-done = f32[32,24,384]{2,1,0:T(8,128)} async-done(((f32[4,24,384]{2,1,0:T(8,128)}), f32[32,24,384]{2,1,0:T(8,128)}) %all-gather.3.cloned.1.call-update) | async-done | bytes 1179664 | tf_op jit(solution)/shard_map/all_gather | solution.py:110
  173.8 2.0 %reduce_sum.29 = f32[4,24,384]{2,1,0:T(8,128)} reduce(f32[8,4,24,384]{3,2,1,0:T(8,128)} %bitcast.52, f32[]{:T(128)} %constant.13.clone.1), dimensions={0}, to_apply=%region_4.5 | reduce | flops 258048 | bytes 1327108 | tf_op jit(solution)/shard_map/reduce_sum | solution.py:110
  175.8 4.6 %all-to-all-start = ((f32[4,24,384]{2,1,0:T(8,128)}), f32[4,24,384]{2,1,0:T(8,128)S(1)}, u32[]{:S(2)}, u32[]{:S(2)}) async-start(f32[4,24,384]{2,1,0:T(8,128)} %reduce_sum.29), calls=%async_computation.1 | async-start | bytes 294912 | tf_op jit(solution)/shard_map/all_to_all | solution.py:111
  180.4 6.6 %all-to-all-done = f32[4,24,384]{2,1,0:T(8,128)S(1)} async-done(((f32[4,24,384]{2,1,0:T(8,128)}), f32[4,24,384]{2,1,0:T(8,128)S(1)}, u32[]{:S(2)}, u32[]{:S(2)}) %all-to-all-start) | async-done | bytes 147488 | tf_op jit(solution)/shard_map/all_to_all | solution.py:111
  187.1 0.7 fusion.49
  (46 shorter events, 3.4 us)
Async XLA Ops:
  6.5 0.7 copy-start
  6.5 88.9 %all-reduce.3.cloned.1.call-start = ((), (), s32[]{:S(2)}) async-start(), calls=%async_computation.2 | async-start | bytes 2097152 | tf_op jit(solution)/shard_map/psum | solution.py:71
  18.8 7.2 %copy-start.1 = (bf16[16,512,160]{1,2,0:T(8,128)(2,1)}, bf16[16,512,160]{1,2,0:T(8,128)(2,1)S(1)}, u32[]{:S(2)}) copy-start(bf16[16,512,160]{1,2,0:T(8,128)(2,1)S(1)} %convert_bitcast_fusion) | copy-start | bytes 7864324
  26.0 7.2 %copy-start.3 = (bf16[16,512,144]{1,2,0:T(8,128)(2,1)}, bf16[16,512,144]{1,2,0:T(8,128)(2,1)S(1)}, u32[]{:S(2)}) copy-start(bf16[16,512,144]{1,2,0:T(8,128)(2,1)S(1)} %convert_bitcast_fusion.2) | copy-start | bytes 7077892
  26.1 8.6 %copy-start.8 = (s32[16]{0:T(128)S(1)}, s32[16]{0:T(128)}, u32[]{:S(2)}) copy-start(s32[16]{0:T(128)} %param.14) | copy-start | bytes 196
  26.1 8.6 %slice-start = ((bf16[16,512,160]{1,2,0:T(8,128)(2,1)}), bf16[16,512,32]{1,2,0:T(8,128)(2,1)S(1)}, s32[]{:S(2)}) async-start(bf16[16,512,160]{1,2,0:T(8,128)(2,1)} %copy-done.1), calls=%async_computation.5 | async-start | bytes 1048576 | tf_op jit(solution)/shard_map/slice | solution.py:68
  33.2 1.4 copy-start.5
  33.2 62.3 %copy-start.2 = (bf16[16,512,160]{1,2,0:T(8,128)(2,1)S(1)}, bf16[16,512,160]{1,2,0:T(8,128)(2,1)}, u32[]{:S(2)}) copy-start(bf16[16,512,160]{1,2,0:T(8,128)(2,1)} %copy-done.1) | copy-start | bytes 7864324
  36.0 98.1 %reduce-scatter.2.cloned.1.call-start = ((), (), s32[]{:S(2)}) async-start(), calls=%async_computation.3 | async-start | bytes 294912 | tf_op jit(solution)/shard_map/reduce_scatter | solution.py:90
  95.5 3.5 %copy-start.4 = (bf16[16,512,144]{1,2,0:T(8,128)(2,1)S(1)}, bf16[16,512,144]{1,2,0:T(8,128)(2,1)}, u32[]{:S(2)}) copy-start(bf16[16,512,144]{1,2,0:T(8,128)(2,1)} %copy-done.3) | copy-start | bytes 7077892
  95.5 3.5 %copy-start.9 = (bf16[16,512,64]{1,2,0:T(8,128)(2,1)S(1)}, bf16[16,512,64]{1,2,0:T(8,128)(2,1)}, u32[]{:S(2)}) copy-start(bf16[16,512,64]{1,2,0:T(8,128)(2,1)} %all-reduce.3.cloned.1.call-done) | copy-start | bytes 3145732
  97.2 2.4 %copy-start.6 = (bf16[16,512,144]{1,2,0:T(8,128)(2,1)S(1)}, bf16[16,512,144]{1,2,0:T(8,128)(2,1)}, u32[]{:S(2)}) copy-start(bf16[16,512,144]{1,2,0:T(8,128)(2,1)} %copy-done.5) | copy-start | bytes 7077892
  99.7 1.7 copy-start.7
  101.3 72.5 %all-gather.3.cloned.1.call-start = ((), (), s32[]{:S(2)}) async-start(), calls=%async_computation.4 | async-start | bytes 1327104 | tf_op jit(solution)/shard_map/all_gather | solution.py:110
  175.8 11.2 %all-to-all-start = ((f32[4,24,384]{2,1,0:T(8,128)}), f32[4,24,384]{2,1,0:T(8,128)S(1)}, u32[]{:S(2)}, u32[]{:S(2)}) async-start(f32[4,24,384]{2,1,0:T(8,128)} %reduce_sum.29), calls=%async_computation.1 | async-start | bytes 294912 | tf_op jit(solution)/shard_map/all_to_all | solution.py:111
Sparse Core Ops, SparseCore 0:
  36.1 59.2 all-reduce.2
  101.4 32.6 reduce-scatter.1
  149.8 23.9 all-gather.2
